TPU v7x, 256 devices: a whole 4x4x8 slice. The times are simulated.
256 devices in a mesh: grp: 2 (over core), seq: 32 (over z, x), head: 4 (over y).
Axes of the slice: x: 4, y: 4, z: 8, core: 2. Of those that a mesh axis runs over, the one named last changes fastest.
Arguments:
- queries: bfloat16 [6144, 64, 128], P('seq', ('grp', 'head')), may hold values from -6 to 6
- keys: bfloat16 [6144, 64, 128], P('seq', ('grp', 'head')), may hold values from -6 to 6
- values: bfloat16 [6144, 64, 128], P('seq', ('grp', 'head')), may hold values from -6 to 6
- documents: int32 [6144], P('seq'), may hold values from 0 to 3, never falling along the last dimension, each value on 1 to 4608 neighbouring positions
- feature_map: float32 [64, 128, 128], P(('grp', 'head')), may hold values from -8 to 8
Outputs:
- teacher_out: bfloat16 [6144, 64, 128], P('seq', ('grp', 'head'))
- student_out: bfloat16 [6144, 64, 128], P('seq', ('grp', 'head'))
- loss: float32 [], replicated
- feature_grad: float32 [64, 128, 128], P(('grp', 'head'))
All inputs are finite; a program needn't handle non-finite values.
Results may differ from a plain program's by a relative error of at most 0.006.
Values may be sent and summed in bfloat16 or wider, within the bound.
A program may use at most 192 MiB of HBM per device.

v0:
```python
import functools
import jax
import jax.numpy as jnp
from jax import lax
from jax.sharding import Mesh
from jax.sharding import PartitionSpec as P

WINDOW = 64
SEQ = ("seq_0", "seq_1")
GRP_SEQ_HEAD = ("grp", "seq_0", "seq_1", "head")
exact_mode = lax.Precision.HIGHEST
masked_value = -1e30


def passed_along(block, axis, distance):
    devices = range(lax.axis_size(axis))
    route = [(i - distance, i) for i in devices if i - distance in devices]
    return lax.ppermute(block, axis, route)


def filled_with(array, identity):
    return jax.tree.map(
        lambda part, zero: jnp.zeros_like(part) + jnp.asarray(zero, part.dtype), array, identity
    )


def carried_in(array, axes, combine, identity, reverse):
    before = start = filled_with(array, identity)
    subtotal = array
    for axis in reversed(axes):
        peers, mine = (lax.axis_size(axis), lax.axis_index(axis))
        pieces = jax.tree.map(lambda part: lax.all_gather(part, axis), subtotal)
        inside, subtotal = (start, start)
        for k in reversed(range(peers)) if reverse else range(peers):
            passed = k > mine if reverse else k < mine
            subtotal = combine(subtotal, jax.tree.map(lambda part: part[k], pieces))
            inside = jax.tree.map(lambda new, old: jnp.where(passed, new, old), subtotal, inside)
        before = combine(inside, before)
    return before


def over_axes(array, axes):
    return functools.reduce(lax.psum, axes, array)


def features(inputs, weights):
    logits = jnp.einsum("rhd,hdf->rhf", inputs, weights, precision=exact_mode)
    return jnp.concatenate(
        [jax.nn.softmax(logits, axis=-1), jax.nn.softmax(-logits, axis=-1)], axis=-1
    )


def join_up(earlier, later):
    merged_tag = jnp.maximum(earlier[0], later[0])
    early_keep = (earlier[0] == merged_tag).astype(earlier[1].dtype)
    late_keep = (later[0] == merged_tag).astype(later[1].dtype)
    return (
        merged_tag,
        early_keep * earlier[1] + late_keep * later[1],
        early_keep * earlier[2] + late_keep * later[2],
    )


def join_down(earlier, later):
    merged_tag = jnp.minimum(earlier[0], later[0])
    early_keep = (earlier[0] == merged_tag).astype(earlier[1].dtype)
    late_keep = (later[0] == merged_tag).astype(later[1].dtype)
    return (
        merged_tag,
        early_keep * earlier[1] + late_keep * later[1],
        early_keep * earlier[2] + late_keep * later[2],
    )


def body(queries, keys, values, documents, feature_map):
    tok_rows, head_count, head_width = queries.shape
    half_feat = feature_map.shape[2] // 2
    score_scale = head_width ** (-0.5)
    seq_place = lax.axis_index(SEQ)
    seq_count = lax.axis_size(SEQ)
    first_row = seq_place * tok_rows
    doc_float = documents.astype(jnp.float32)
    doc_marks = (documents + 1).astype(jnp.bfloat16)
    query_pos = first_row + jnp.arange(tok_rows)
    key_piece = lax.all_gather(keys, SEQ, axis=0, tiled=True)
    value_piece = lax.all_gather(values, SEQ, axis=0, tiled=True)
    mark_piece = lax.all_gather(doc_marks, SEQ, axis=0, tiled=True)
    key_pos = jnp.arange(key_piece.shape[0])
    same_doc = mark_piece.astype(jnp.float32)[None, :] - 1.0 == doc_float[:, None]
    allowed = (same_doc & (key_pos[None, :] <= query_pos[:, None]))[:, None, :]
    scores = (
        jnp.einsum("ihd,jhd->ihj", queries, key_piece, preferred_element_type=jnp.float32)
        * score_scale
    )
    scores = jnp.where(allowed, scores, masked_value)
    row_max = jnp.full((tok_rows, head_count), masked_value, jnp.float32)
    new_max = jnp.maximum(row_max, jnp.max(scores, axis=-1))
    probabilities = jnp.where(allowed, jnp.exp(scores - new_max[:, :, None]), 0.0)
    totals = jnp.sum(probabilities, axis=-1)
    numerator = jnp.einsum(
        "ihj,jhd->ihd",
        probabilities.astype(jnp.bfloat16),
        value_piece,
        preferred_element_type=jnp.float32,
    )
    row_max, totals, numerator = (new_max, totals, numerator)
    teacher_out = (numerator / totals[:, :, None]).astype(jnp.bfloat16)
    target = teacher_out.astype(jnp.float32)
    halo_keys, halo_values, halo_marks = passed_along(
        (keys[tok_rows - WINDOW :], values[tok_rows - WINDOW :], doc_marks[tok_rows - WINDOW :]),
        SEQ,
        1,
    )
    key_joined = jnp.concatenate([halo_keys, keys], axis=0)
    key_float = key_joined.astype(jnp.float32)
    value_float = jnp.concatenate([halo_values, values], axis=0).astype(jnp.float32)
    doc_all = jnp.concatenate([halo_marks.astype(jnp.float32) - 1.0, doc_float], axis=0)
    query_float = queries.astype(jnp.float32)
    distance = jnp.arange(tok_rows)[:, None] + WINDOW - jnp.arange(tok_rows + WINDOW)[None, :]
    same_doc = doc_float[:, None] == doc_all[None, :]
    in_window = same_doc & (distance >= 0) & (distance < WINDOW)
    beyond = same_doc & (distance >= WINDOW)
    scores = (
        jnp.einsum("ihd,jhd->hij", queries, key_joined, preferred_element_type=jnp.float32)
        * score_scale
    )
    window_row = jnp.max(jnp.where(in_window[None], scores, masked_value), axis=-1, keepdims=True)
    window_weight = jnp.where(in_window[None], jnp.exp(scores - window_row), 0.0)
    elem_keys = key_float[:tok_rows]
    elem_values = value_float[:tok_rows]
    elem_docs = doc_all[:tok_rows]
    elem_tag = elem_docs[tok_rows - 1]
    in_tail = (elem_docs == elem_tag).astype(jnp.float32)

    def element(weights):
        masked_feat = features(elem_keys, weights[:, :, half_feat:]) * in_tail[:, None, None]
        return (
            jnp.einsum("jhf,jhd->hfd", masked_feat, elem_values, precision=exact_mode),
            jnp.sum(masked_feat, axis=0),
        )

    (elem_state, elem_norm), element_pullback = jax.vjp(element, feature_map)
    blank_state = jnp.zeros_like(elem_state)
    blank_norm = jnp.zeros_like(elem_norm)
    tag_in, state_in, norm_in = carried_in(
        (elem_tag, elem_state, elem_norm),
        SEQ,
        join_up,
        (jnp.float32(-2.0), blank_state, blank_norm),
        False,
    )
    uses_state = (doc_float == tag_in).astype(jnp.float32)[:, None]
    normaliser = 1.0 / (tok_rows * seq_count * head_count * lax.axis_size(("grp", "head")))

    def local_loss(weights, state, norm):
        query_feat = features(query_float, weights[:, :, :half_feat])
        key_feat = features(key_float, weights[:, :, half_feat:])
        linear = jnp.where(
            beyond[None],
            jnp.einsum("ihf,jhf->hij", query_feat, key_feat, precision=exact_mode),
            0.0,
        )
        weight = window_weight + linear
        numer_sum = jnp.einsum("hij,jhd->ihd", weight, value_float, precision=exact_mode)
        numer_sum = numer_sum + uses_state[:, :, None] * jnp.einsum(
            "ihf,hfd->ihd", query_feat, state, precision=exact_mode
        )
        denominator = jnp.sum(weight, axis=-1).T + uses_state * jnp.einsum(
            "ihf,hf->ih", query_feat, norm, precision=exact_mode
        )
        output = numer_sum / denominator[:, :, None]
        return (jnp.sum(jnp.square(output - target)) * normaliser, output)

    local_part, local_pullback, output = jax.vjp(
        local_loss, feature_map, state_in, norm_in, has_aux=True
    )
    grad_direct, grad_state, grad_norm = local_pullback(jnp.ones_like(local_part))
    back_tag, carried_state, carried_norm = carried_in(
        (tag_in, grad_state, grad_norm),
        SEQ,
        join_down,
        (jnp.float32(1000000000.0), blank_state, blank_norm),
        True,
    )
    total_grad = grad_direct + element_pullback((carried_state, carried_norm))[0]
    feature_grad = over_axes(total_grad, SEQ)
    loss_total = jax.tree.map(lambda part: over_axes(part, GRP_SEQ_HEAD), local_part)
    return (teacher_out, output.astype(jnp.bfloat16), loss_total, feature_grad)


def solution(mesh):
    split = Mesh(
        mesh.devices.reshape(mesh.shape["grp"], 8, 4, mesh.shape["head"]),
        ("grp", "seq_0", "seq_1", "head"),
    )
    return jax.shard_map(
        body,
        mesh=split,
        in_specs=(
            P(SEQ, ("grp", "head"), None),
            P(SEQ, ("grp", "head"), None),
            P(SEQ, ("grp", "head"), None),
            P(SEQ),
            P(("grp", "head"), None, None),
        ),
        out_specs=(
            P(SEQ, ("grp", "head"), None),
            P(SEQ, ("grp", "head"), None),
            P(),
            P(("grp", "head"), None, None),
        ),
        check_vma=False,
    )
```

profile of v0, /device:TPU:8, one launch (start us, length us, event | category | flops | bytes accessed | tf_op | source)
XLA Modules:
  0.0 640.9 jit_solution(11608733308166562102)
XLA Ops:
  7.3 1.1 copy.34
  8.4 3.4 collective-permute-start.2
  12.6 3.4 collective-permute-start.1
  16.0 1.1 copy.36
  17.1 3.1 collective-permute-start
  20.8 1.2 slice_dynamic-update-slice_fusion
  23.0 1.0 convolution_bitcast_fusion.1
  27.2 1.5 fusion.37
  28.8 11.1 %all-reduce.4 = f32[4]{0:T(128)S(1)} all-reduce(f32[4]{0:T(128)S(1)} %get-tuple-element.28), channel_id=1, replica_groups=mesh['grp'=2,'seq_0'=8,'seq_1'=4,'head'=4] {'seq_1'}, use_global_device_ids=true, to_apply=%add.4 | all-reduce | flops 4 | bytes 32
  45.8 18.7 %all-gather.19.cloned.1.call-done = f32[32,128,128]{2,1,0:T(8,128)} async-done(((f32[8,128,128]{2,1,0:T(8,128)}), f32[32,128,128]{2,1,0:T(8,128)}) %all-gather.19.cloned.1.call-update) | async-done | bytes 2097168 | tf_op jit(solution)/shard_map/all_gather | solution.py:32
  64.5 2.5 fusion.75
  69.8 17.9 %all-reduce.5 = f32[8]{0:T(128)S(1)} all-reduce(f32[8]{0:T(128)S(1)} %dynamic-update-slice.2), channel_id=1, replica_groups=mesh['grp'=2,'seq_0'=8,'seq_1'=4,'head'=4] {'seq_0'}, use_global_device_ids=true, to_apply=%add.5 | all-reduce | flops 8 | bytes 64
  100.3 142.1 %all-reduce.3 = bf16[6144]{0:T(1024)(128)(2,1)S(1)} all-reduce(bf16[6144]{0:T(1024)(128)(2,1)S(1)} %dynamic-update-slice), channel_id=1, replica_groups=mesh['grp'=2,'seq_0'=8,'seq_1'=4,'head'=4] {'seq_0','seq_1'}, use_global_device_ids=true, to_apply=%add.3 | all-reduce | flops 6144 | bytes 24576
  243.3 0.9 fusion.273
  246.1 1.0 fusion.13
  247.6 12.0 %all-gather.1 = f32[32,128]{1,0:T(8,128)S(1)} all-gather(f32[8,128]{1,0:T(8,128)S(1)} %fusion.36), channel_id=3, replica_groups=mesh['grp'=2,'seq_0'=8,'seq_1'=4,'head'=4] {'seq_1'}, dimensions={0}, use_global_device_ids=true | all-gather | bytes 20480 | tf_op jit(solution)/shard_map/all_gather | solution.py:32
  259.6 25.2 %all_gather.81 = f32[8,8,128]{2,1,0:T(8,128)S(1)} all-gather(f32[1,8,128]{2,1,0:T(8,128)S(1)} %fusion.245), channel_id=1, replica_groups=mesh['grp'=2,'seq_0'=8,'seq_1'=4,'head'=4] {'seq_0'}, dimensions={0}, use_global_device_ids=true | all-gather | bytes 36864 | tf_op jit(solution)/shard_map/all_gather | solution.py:32
  284.8 0.9 convolution_bitcast_fusion.2
  288.4 2.0 fusion.35
  291.5 2.0 fusion.277
  293.5 4.0 fusion.67
  298.3 2.7 convolution_multiply_fusion.1
  301.1 18.7 %fusion.7 = (f32[192,8]{0,1:T(8,128)S(1)}, f32[8,6144,192]{1,2,0:T(8,128)}) fusion(pred[192,6144]{1,0:T(8,128)(4,1)S(1)} %fusion.13, bf16[6144,8,128]{2,0,1:T(8,128)(2,1)} %all-gather.11.cloned.1.call-done, bf16[192,8,128]{2,1,0:T(8,128)(2,1)S(1)} %copy-done), kind=kOutput, calls=%fused_computation.9 | convolution fusion | flops 2444229120 | bytes 51910656 | tf_op jit(solution)/shard_map/ihd,jhd->ihj/dot_general | solution.py:92
  319.7 18.9 %fusion.8 = f32[192,8]{0,1:T(8,128)S(1)} fusion(f32[8,6144,192]{1,2,0:T(8,128)} %get-tuple-element.71, f32[192,8]{0,1:T(8,128)S(1)} %broadcast_maximum_fusion, pred[192,6144]{1,0:T(8,128)(4,1)S(1)} %fusion.13), kind=kLoop, calls=%fused_computation.10 | loop fusion | flops 47184384 | bytes 38940672 | tf_op jit(solution)/shard_map/reduce_sum | solution.py:99
  338.6 24.1 %all-gather.13.cloned.1.call-done = bf16[6144,8,128]{2,0,1:T(8,128)(2,1)} async-done(((bf16[192,8,128]{2,0,1:T(8,128)(2,1)}), bf16[6144,8,128]{2,0,1:T(8,128)(2,1)}) %all-gather.13.cloned.1.call-update) | async-done | bytes 12582928 | tf_op jit(solution)/shard_map/all_gather | solution.py:86
  362.8 21.5 %fusion.10 = f32[8,192,128]{2,1,0:T(8,128)} fusion(bf16[6144,8,128]{2,0,1:T(8,128)(2,1)} %all-gather.13.cloned.1.call-done, f32[8,6144,192]{1,2,0:T(8,128)} %get-tuple-element.71, f32[192,8]{0,1:T(8,128)S(1)} %broadcast_maximum_fusion, pred[192,6144]{1,0:T(8,128)(4,1)S(1)} %fusion.13), kind=kOutput, calls=%fused_computation.12 | convolution fusion | flops 2463105024 | bytes 52303872 | tf_op jit(solution)/shard_map/ihj,jhd->ihd/dot_general | solution.py:100
  384.3 3.7 fusion.40
  388.5 2.0 fusion.44
  391.4 8.6 %all-reduce.6 = f32[4]{0:T(128)S(1)} all-reduce(f32[4]{0:T(128)S(1)} %dynamic-update-slice.3), channel_id=1, replica_groups=mesh['grp'=2,'seq_0'=8,'seq_1'=4,'head'=4] {'seq_1'}, use_global_device_ids=true, to_apply=%add.6 | all-reduce | flops 4 | bytes 32
  405.4 15.7 %all-gather.21.cloned.1.call-done = f32[32,128,128]{2,1,0:T(8,128)} async-done(((f32[8,128,128]{2,1,0:T(8,128)}), f32[32,128,128]{2,1,0:T(8,128)}) %all-gather.21.cloned.1.call-update) | async-done | bytes 2097168 | tf_op jit(solution)/shard_map/all_gather | solution.py:32
  421.1 2.5 fusion.60
  425.8 3.0 psum.42
  428.7 18.6 %all-reduce.8 = (f32[]{:T(128)}, f32[8]{0:T(128)S(1)}) all-reduce(f32[]{:T(128)} %psum.42, f32[8]{0:T(128)S(1)} %dynamic-update-slice.4), channel_id=1, replica_groups=mesh['grp'=2,'seq_0'=8,'seq_1'=4,'head'=4] {'seq_0'}, use_global_device_ids=true, to_apply=%region_19.20 | all-reduce | flops 9 | bytes 72 | tf_op jit(solution)/shard_map/psum | solution.py:43
  457.9 2.0 add_select_fusion
  460.0 1.9 fusion.34
  461.9 1.8 fusion.21
  464.0 1.3 convolution_bitcast_fusion
  465.6 0.9 fusion.213
  466.5 12.0 %all-gather.2 = f32[32,128]{1,0:T(8,128)S(1)} all-gather(f32[8,128]{1,0:T(8,128)S(1)} %bitcast.225), channel_id=4, replica_groups=mesh['grp'=2,'seq_0'=8,'seq_1'=4,'head'=4] {'seq_1'}, dimensions={0}, use_global_device_ids=true | all-gather | bytes 20480 | tf_op jit(solution)/shard_map/all_gather | solution.py:32
  478.5 24.7 %all_gather.88 = f32[8,8,128]{2,1,0:T(8,128)S(1)} all-gather(f32[1,8,128]{2,1,0:T(8,128)S(1)} %fusion.230), channel_id=1, replica_groups=mesh['grp'=2,'seq_0'=8,'seq_1'=4,'head'=4] {'seq_0'}, dimensions={0}, use_global_device_ids=true | all-gather | bytes 36864 | tf_op jit(solution)/shard_map/all_gather | solution.py:32
  505.7 4.1 fusion.19
  511.7 71.1 %all-reduce.12.cloned.1.call-done = f32[8,128,128]{1,2,0:T(8,128)} async-done(((f32[8,128,128]{1,2,0:T(8,128)}), f32[8,128,128]{1,2,0:T(8,128)}) %all-reduce.12.cloned.1.call-update) | async-done | bytes 524304 | tf_op jit(solution)/shard_map/psum | solution.py:43
  582.9 11.1 %psum.44 = f32[]{:T(128)} all-reduce(f32[]{:T(128)} %get-tuple-element.20), channel_id=1, replica_groups=mesh['grp'=2,'seq_0'=8,'seq_1'=4,'head'=4] {'seq_1'}, use_global_device_ids=true, to_apply=%region_20.21 | all-reduce | flops 1 | bytes 8 | tf_op jit(solution)/shard_map/psum | solution.py:43
  593.9 9.2 %psum.45 = f32[]{:T(128)} all-reduce(f32[]{:T(128)} %psum.44), channel_id=1, replica_groups=mesh['grp'=2,'seq_0'=8,'seq_1'=4,'head'=4] {'head'}, use_global_device_ids=true, to_apply=%region_21.22 | all-reduce | flops 1 | bytes 8 | tf_op jit(solution)/shard_map/psum | solution.py:43
  603.2 1.0 copy.56
  604.2 1.0 copy.57
  605.2 26.6 %all-reduce.14.cloned.1.call-done = f32[8,128,128]{1,2,0:T(8,128)} async-done(((f32[8,128,128]{1,2,0:T(8,128)}), f32[8,128,128]{1,2,0:T(8,128)}) %all-reduce.14.cloned.1.call-update) | async-done | bytes 524304 | tf_op jit(solution)/shard_map/psum | solution.py:43
  631.8 2.0 copy.58
  (200 shorter events, 26.8 us)
Async XLA Ops:
  7.2 235.3 %copy-start = (bf16[192,8,128]{2,1,0:T(8,128)(2,1)S(1)}, bf16[192,8,128]{2,1,0:T(8,128)(2,1)}, u32[]{:S(2)}) copy-start(bf16[192,8,128]{2,1,0:T(8,128)(2,1)} %param.5) | copy-start | bytes 1179652
  7.2 13.0 %copy-start.53 = (u32[256]{0:T(256)S(1)}, u32[256]{0:T(256)}, u32[]{:S(2)}) copy-start(u32[256]{0:T(256)} %constant.93) | copy-start | bytes 3076
  7.2 15.7 %copy-start.31 = (bf16[192,8,128]{2,1,0:T(8,128)(2,1)S(1)}, bf16[192,8,128]{2,1,0:T(8,128)(2,1)}, u32[]{:S(2)}) copy-start(bf16[192,8,128]{2,1,0:T(8,128)(2,1)} %param.6) | copy-start | bytes 1179652
  7.2 15.8 %copy-start.11 = (f32[8,128,128]{2,1,0:T(8,128)S(1)}, f32[8,128,128]{2,1,0:T(8,128)}, u32[]{:S(2)}) copy-start(f32[8,128,128]{2,1,0:T(8,128)} %param.9) | copy-start | bytes 1572868
  7.2 57.3 %all-gather.19.cloned.1.call-start = ((), (), s32[]{:S(2)}) async-start(), calls=%async_computation.6 | async-start | bytes 2621440 | tf_op jit(solution)/shard_map/all_gather | solution.py:32
  8.4 16.6 %copy-start.25 = (bf16[192,8,128]{2,0,1:T(8,128)(2,1)}, bf16[192,8,128]{2,0,1:T(8,128)(2,1)S(1)}, u32[]{:S(2)}) copy-start(bf16[192,8,128]{2,0,1:T(8,128)(2,1)S(1)} %copy.34) | copy-start | bytes 1179652
  8.4 14.4 %collective-permute-start.2 = (bf16[64,8,128]{2,0,1:T(8,128)(2,1)S(1)}, bf16[64,8,128]{2,0,1:T(8,128)(2,1)S(1)}, u32[]{:S(2)}, u32[]{:S(2)}) collective-permute-start(bf16[64,8,128]{2,0,1:T(8,128)(2,1)S(1)} %slice.344), channel_id=1, source_target_pairs={{0,4},{4,8},{8,12},{12,16},{16,20},{20,24},{24,28},{28,32},{32,36}... | collective-permute-start | bytes 393224 | tf_op jit(solution)/shard_map/ppermute | solution.py:18
  12.6 10.2 %copy-start.44 = (f32[192]{0:T(256)}, f32[192]{0:T(256)S(1)}, u32[]{:S(2)}) copy-start(f32[192]{0:T(256)S(1)} %get-tuple-element.31) | copy-start | bytes 2308
  12.6 9.5 %collective-permute-start.1 = (bf16[64]{0:T(256)(128)(2,1)S(1)}, bf16[64]{0:T(256)(128)(2,1)S(1)}, u32[]{:S(2)}, u32[]{:S(2)}) collective-permute-start(bf16[64]{0:T(256)(128)(2,1)S(1)} %slice.247), channel_id=1, source_target_pairs={{0,4},{4,8},{8,12},{12,16},{16,20},{20,24},{24,28},{28,32},{32,36}... | collective-permute-start | bytes 392 | tf_op jit(solution)/shard_map/ppermute | solution.py:18
  17.1 8.8 %copy-start.26 = (bf16[192,8,128]{2,0,1:T(8,128)(2,1)}, bf16[192,8,128]{2,0,1:T(8,128)(2,1)S(1)}, u32[]{:S(2)}) copy-start(bf16[192,8,128]{2,0,1:T(8,128)(2,1)S(1)} %copy.36) | copy-start | bytes 1179652
  17.1 8.8 %collective-permute-start = (bf16[64,8,128]{2,0,1:T(8,128)(2,1)S(1)}, bf16[64,8,128]{2,0,1:T(8,128)(2,1)S(1)}, u32[]{:S(2)}, u32[]{:S(2)}) collective-permute-start(bf16[64,8,128]{2,0,1:T(8,128)(2,1)S(1)} %slice.343), channel_id=1, source_target_pairs={{0,4},{4,8},{8,12},{12,16},{16,20},{20,24},{24,28},{28,32},{32,36}... | collective-permute-start | bytes 393224 | tf_op jit(solution)/shard_map/ppermute | solution.py:18
  22.8 3.9 copy-start.46
  23.0 2.9 copy-start.32
  28.7 39.7 %copy-start.52 = (u32[256]{0:T(256)S(1)}, u32[256]{0:T(256)}, u32[]{:S(2)}) copy-start(u32[256]{0:T(256)} %constant.98) | copy-start | bytes 3076
  28.7 264.8 %all-gather.15.cloned.1.call-start = ((), (), s32[]{:S(2)}) async-start(), calls=%async_computation.2 | async-start | bytes 4718592 | tf_op jit(solution)/shard_map/all_gather | solution.py:32
  40.6 58.2 %copy-start.51 = (u32[256]{0:T(256)S(1)}, u32[256]{0:T(256)}, u32[]{:S(2)}) copy-start(u32[256]{0:T(256)} %constant.88) | copy-start | bytes 3076
  45.8 196.6 %copy-start.50 = (s32[192]{0:T(256)S(1)}, s32[192]{0:T(256)}, u32[]{:S(2)}) copy-start(s32[192]{0:T(256)} %param.8) | copy-start | bytes 2308
  67.0 234.1 %all-gather.11.cloned.1.call-start = ((), (), s32[]{:S(2)}) async-start(), calls=%async_computation | async-start | bytes 12976128 | tf_op jit(solution)/shard_map/all_gather | solution.py:85
  67.8 295.0 %all-gather.13.cloned.1.call-start = ((), (), s32[]{:S(2)}) async-start(), calls=%async_computation.1 | async-start | bytes 12976128 | tf_op jit(solution)/shard_map/all_gather | solution.py:86
  68.3 352.8 %all-gather.21.cloned.1.call-start = ((), (), s32[]{:S(2)}) async-start(), calls=%async_computation.7 | async-start | bytes 2621440 | tf_op jit(solution)/shard_map/all_gather | solution.py:32
  243.3 2.8 copy-start.45
  244.3 2.9 copy-start.49
  244.3 3.1 copy-start.8
  244.3 3.1 copy-start.10
  244.3 3.1 copy-start.47
  246.0 38.8 %copy-start.12 = (f32[8,128,128]{2,1,0:T(8,128)S(1)}, f32[8,128,128]{2,1,0:T(8,128)}, u32[]{:S(2)}) copy-start(f32[8,128,128]{2,1,0:T(8,128)} %param.9) | copy-start | bytes 1572868
  286.6 142.1 %copy-start.38 = (f32[256,8]{0,1:T(8,128)}, f32[256,8]{0,1:T(8,128)S(1)}, u32[]{:S(2)}) copy-start(f32[256,8]{0,1:T(8,128)S(1)} %get-tuple-element.64) | copy-start | bytes 24580
  287.5 141.2 %copy-start.40 = (f32[256,8]{0,1:T(8,128)}, f32[256,8]{0,1:T(8,128)S(1)}, u32[]{:S(2)}) copy-start(f32[256,8]{0,1:T(8,128)S(1)} %get-tuple-element.66) | copy-start | bytes 24580
  287.6 2.8 copy-start.1
  287.7 2.8 copy-start.3
  362.8 21.5 %copy-start.28 = (bf16[256,8,128]{2,0,1:T(8,128)(2,1)S(1)}, bf16[256,8,128]{2,0,1:T(8,128)(2,1)}, u32[]{:S(2)}) copy-start(bf16[256,8,128]{2,0,1:T(8,128)(2,1)} %copy-done.27) | copy-start | bytes 1572868
  362.8 21.5 %copy-start.33 = (f32[8,192,256]{2,1,0:T(8,128)S(1)}, f32[8,192,256]{2,1,0:T(8,128)}, u32[]{:S(2)}) copy-start(f32[8,192,256]{2,1,0:T(8,128)} %get-tuple-element.69) | copy-start | bytes 4718596
  362.8 21.5 %copy-start.34 = (f32[8,128,192]{1,2,0:T(8,128)S(1)}, f32[8,128,192]{1,2,0:T(8,128)}, u32[]{:S(2)}) copy-start(f32[8,128,192]{1,2,0:T(8,128)} %convolution_multiply_fusion.1) | copy-start | bytes 2359300
  384.3 3.7 copy-start.35
  390.5 114.6 %all-gather.17.cloned.1.call-start = ((), (), s32[]{:S(2)}) async-start(), calls=%async_computation.3 | async-start | bytes 4718592 | tf_op jit(solution)/shard_map/all_gather | solution.py:32
  423.6 36.3 %copy-start.2 = (f32[256,8,64]{0,2,1:T(8,128)S(1)}, f32[256,8,64]{0,2,1:T(8,128)}, u32[]{:S(2)}) copy-start(f32[256,8,64]{0,2,1:T(8,128)} %copy-done.1) | copy-start | bytes 1572868
  423.6 159.2 %all-reduce.12.cloned.1.call-start = ((), (), s32[]{:S(2)}) async-start(), calls=%async_computation.4 | async-start | bytes 1048576 | tf_op jit(solution)/shard_map/psum | solution.py:43
  457.9 2.0 copy-start.4
  459.9 1.9 copy-start.6
  461.9 1.8 copy-start.18
  461.9 1.8 copy-start.20
  505.1 4.8 copy-start.14
  505.1 4.8 copy-start.16
  505.7 4.2 copy-start.42
  505.7 4.2 copy-start.43
  510.8 92.4 %copy-start.37 = (bf16[192,8,128]{2,0,1:T(8,128)(2,1)S(1)}, bf16[192,8,128]{2,0,1:T(8,128)(2,1)}, u32[]{:S(2)}) copy-start(bf16[192,8,128]{2,0,1:T(8,128)(2,1)} %get-tuple-element.22) | copy-start | bytes 1179652
  510.8 93.4 %copy-start.36 = (bf16[192,8,128]{2,0,1:T(8,128)(2,1)S(1)}, bf16[192,8,128]{2,0,1:T(8,128)(2,1)}, u32[]{:S(2)}) copy-start(bf16[192,8,128]{2,0,1:T(8,128)(2,1)} %get-tuple-element.25) | copy-start | bytes 1179652
  511.7 120.1 %all-reduce.14.cloned.1.call-start = ((), (), s32[]{:S(2)}) async-start(), calls=%async_computation.5 | async-start | bytes 1048576 | tf_op jit(solution)/shard_map/psum | solution.py:43
  (17 other events, 16.2 us)
Sparse Core Ops, SparseCore 0:
  28.8 35.6 all-gather.18
  67.1 54.9 all-gather.14
  125.3 118.4 all-gather.10
  246.8 115.8 all-gather.12
  390.7 30.3 all-gather.20
  423.7 55.0 all-gather.16
  511.8 71.0 all-reduce.11
  585.2 46.5 all-reduce.13
where the time goes:
time: 647 us; the launch traced here: 641 us
  blocking collectives  295 us (46%)
  waiting for transfers between devices  158 us (24%)
  matrix products  69.9 us (11%)
  between operations  47.1 us (7%)
  other arithmetic  41.8 us (6%)
  local copies, waits for them, and re-layouts  18.9 us (3%)
  starting transfers between devices  10.2 us (2%)
    unnamed x4, blocking collectives  180 us
    psum x2, waiting for transfers between devices, over_axes(): return functools.reduce(lax.psum, axes, array)  97.7 us
    all_gather x4, blocking collectives, carried_in(): pieces = jax.tree.map(lambda part: lax.all_gather(part, axis), subtotal)  73.9 us
    psum x4, blocking collectives, over_axes(): return functools.reduce(lax.psum, axes, array)  41.8 us
    all_gather x4, waiting for transfers between devices, carried_in(): pieces = jax.tree.map(lambda part: lax.all_gather(part, axis), subtotal)  34.4 us
    all_gather x1, waiting for transfers between devices, body(): value_piece = lax.all_gather(values, SEQ, axis=0, tiled=True)  24.1 us
    dot_general x1, matrix products, body(): jnp.einsum('ihj,jhd->ihd', probabilities.astype(jnp.bfloat16), value_piec...  21.5 us
    reduce_sum x1, other arithmetic, body(): totals = jnp.sum(probabilities, axis=-1)  18.9 us
  transfers between devices with their start and end apart: 11, of which 5 were waited for; matrix products, arithmetic and copies ran while one was open for 13% of the time, Pallas kernels for 0%

commit v1 on v0

--- a/solution.py
+++ b/solution.py
@@ -83,7 +83,9 @@
     doc_marks = (documents + 1).astype(jnp.bfloat16)
     query_pos = first_row + jnp.arange(tok_rows)
     key_piece = lax.all_gather(keys, SEQ, axis=0, tiled=True)
-    value_piece = lax.all_gather(values, SEQ, axis=0, tiled=True)
+    value_piece = jnp.concatenate(
+        lax.all_to_all(jnp.stack([values] * lax.axis_size(SEQ)), SEQ, 0, 0), axis=0
+    )
     mark_piece = lax.all_gather(doc_marks, SEQ, axis=0, tiled=True)
     key_pos = jnp.arange(key_piece.shape[0])
     same_doc = mark_piece.astype(jnp.float32)[None, :] - 1.0 == doc_float[:, None]

time: 647 us -> 1020 us (1.58)
  blocking collectives: 295 us -> 656 us
  waiting for transfers between devices: 158 us -> 135 us
  local copies, waits for them, and re-layouts: 18.9 us -> 39.6 us
    unnamed x4, blocking collectives: 180 us -> 538 us
    all_gather x1 -> x0, waiting for transfers between devices: 24.1 us -> none  [body(): value_piece = lax.all_gather(values, SEQ, axis=0, tiled=True)]
    all_to_all x0 -> x1, local copies, waits for them, and re-layouts: none -> 11.8 us  [body(): lax.all_to_all(jnp.stack([values] * lax.axis_size(SEQ)), SEQ, 0, 0)]
  transfers between devices with their start and end apart: 11 -> 11, of which waited for: 5 -> 4; matrix products, arithmetic and copies ran while one was open for 13% -> 9% of each run, Pallas kernels for 0% -> 0%
where the time goes in v1:
time: 1020 us; the launch traced here: 1010 us
  blocking collectives  656 us (64%)
  waiting for transfers between devices  135 us (13%)
  matrix products  74.4 us (7%)
  between operations  47 us (5%)
  other arithmetic  41.1 us (4%)
  local copies, waits for them, and re-layouts  39.6 us (4%)
  starting transfers between devices  19 us (2%)
    unnamed x4, blocking collectives  538 us
    psum x2, waiting for transfers between devices, over_axes(): return functools.reduce(lax.psum, axes, array)  97.7 us
    all_gather x4, blocking collectives, carried_in(): pieces = jax.tree.map(lambda part: lax.all_gather(part, axis), subtotal)  76.1 us
    psum x4, blocking collectives, over_axes(): return functools.reduce(lax.psum, axes, array)  41.9 us
    all_gather x4, waiting for transfers between devices, carried_in(): pieces = jax.tree.map(lambda part: lax.all_gather(part, axis), subtotal)  36.7 us
    dot_general x1, matrix products, body(): jnp.einsum('ihj,jhd->ihd', probabilities.astype(jnp.bfloat16), value_piec...  21.5 us
  transfers between devices with their start and end apart: 11, of which 4 were waited for; matrix products, arithmetic and copies ran while one was open for 9% of the time, Pallas kernels for 0%

profile of v1, /device:TPU:8, one launch (start us, length us, event | category | flops | bytes accessed | tf_op | source)
XLA Modules:
  0.0 1012.4 jit_solution(4221319601365643182)
XLA Ops:
  7.2 1.1 copy.34
  8.4 3.4 collective-permute-start.2
  12.6 3.4 collective-permute-start.1
  17.1 3.1 collective-permute-start
  20.2 1.3 dynamic-slice.1
  21.5 1.2 slice_dynamic-update-slice_fusion
  23.5 1.1 constant_dynamic-update-slice_fusion.2
  24.6 2.1 convolution_bitcast_fusion.1
  30.3 1.5 fusion.37
  31.9 11.1 %all-reduce.4 = f32[4]{0:T(128)S(1)} all-reduce(f32[4]{0:T(128)S(1)} %get-tuple-element.28), channel_id=1, replica_groups=mesh['grp'=2,'seq_0'=8,'seq_1'=4,'head'=4] {'seq_1'}, use_global_device_ids=true, to_apply=%add.4 | all-reduce | flops 4 | bytes 32
  48.7 19.0 %all-gather.16.cloned.1.call-done = f32[32,128,128]{2,1,0:T(8,128)} async-done(((f32[8,128,128]{2,1,0:T(8,128)}), f32[32,128,128]{2,1,0:T(8,128)}) %all-gather.16.cloned.1.call-update) | async-done | bytes 2097168 | tf_op jit(solution)/shard_map/all_gather | solution.py:32
  67.7 2.5 fusion.75
  70.9 7.7 stack.2
  78.6 8.8 all-to-all-start
  88.8 381.6 %all-reduce.5 = f32[8]{0:T(128)S(1)} all-reduce(f32[8]{0:T(128)S(1)} %dynamic-update-slice.2), channel_id=1, replica_groups=mesh['grp'=2,'seq_0'=8,'seq_1'=4,'head'=4] {'seq_0'}, use_global_device_ids=true, to_apply=%add.5 | all-reduce | flops 8 | bytes 64
  482.5 137.7 %all-reduce.3 = bf16[6144]{0:T(1024)(128)(2,1)S(1)} all-reduce(bf16[6144]{0:T(1024)(128)(2,1)S(1)} %dynamic-update-slice), channel_id=1, replica_groups=mesh['grp'=2,'seq_0'=8,'seq_1'=4,'head'=4] {'seq_0','seq_1'}, use_global_device_ids=true, to_apply=%add.3 | all-reduce | flops 6144 | bytes 24576
  625.1 1.4 fusion.36
  626.6 12.0 %all-gather.1 = f32[32,128]{1,0:T(8,128)S(1)} all-gather(f32[8,128]{1,0:T(8,128)S(1)} %fusion.36), channel_id=3, replica_groups=mesh['grp'=2,'seq_0'=8,'seq_1'=4,'head'=4] {'seq_1'}, dimensions={0}, use_global_device_ids=true | all-gather | bytes 20480 | tf_op jit(solution)/shard_map/all_gather | solution.py:32
  638.6 27.4 %all_gather.77 = f32[8,8,128]{2,1,0:T(8,128)S(1)} all-gather(f32[1,8,128]{2,1,0:T(8,128)S(1)} %fusion.245), channel_id=1, replica_groups=mesh['grp'=2,'seq_0'=8,'seq_1'=4,'head'=4] {'seq_0'}, dimensions={0}, use_global_device_ids=true | all-gather | bytes 36864 | tf_op jit(solution)/shard_map/all_gather | solution.py:32
  666.0 2.0 convolution_bitcast_fusion.2
  670.5 2.0 fusion.35
  673.7 2.0 fusion.277
  675.7 3.7 fusion.67
  680.2 2.7 convolution_multiply_fusion.1
  682.9 18.0 %fusion.7 = (f32[192,8]{0,1:T(8,128)S(1)}, f32[8,6144,192]{1,2,0:T(8,128)}) fusion(pred[192,6144]{1,0:T(8,128)(4,1)S(1)} %fusion.13, bf16[6144,8,128]{2,0,1:T(8,128)(2,1)} %all-gather.10.cloned.1.call-done, bf16[192,8,128]{2,1,0:T(8,128)(2,1)S(1)} %copy-done), kind=kOutput, calls=%fused_computation.9 | convolution fusion | flops 2444229120 | bytes 51910656 | tf_op jit(solution)/shard_map/ihd,jhd->ihj/dot_general | solution.py:94
  700.9 18.6 %fusion.8 = f32[192,8]{0,1:T(8,128)S(1)} fusion(f32[8,6144,192]{1,2,0:T(8,128)} %get-tuple-element.71, f32[192,8]{0,1:T(8,128)S(1)} %broadcast_maximum_fusion, pred[192,6144]{1,0:T(8,128)(4,1)S(1)} %fusion.13), kind=kLoop, calls=%fused_computation.10 | loop fusion | flops 47184384 | bytes 38940672 | tf_op jit(solution)/shard_map/reduce_sum | solution.py:101
  719.5 11.8 %copy.37 = bf16[32,192,8,128]{3,1,0,2:T(8,128)(2,1)} copy(bf16[32,192,8,128]{3,1,2,0:T(8,128)(2,1)} %all-to-all-done) | data formatting | bytes 25165824 | tf_op jit(solution)/shard_map/all_to_all | solution.py:87
  731.3 21.5 %fusion.10 = f32[8,192,128]{2,1,0:T(8,128)} fusion(bf16[6144,8,128]{2,0,1:T(8,128)(2,1)} %bitcast.223, f32[8,6144,192]{1,2,0:T(8,128)} %get-tuple-element.71, f32[192,8]{0,1:T(8,128)S(1)} %broadcast_maximum_fusion, pred[192,6144]{1,0:T(8,128)(4,1)S(1)} %fusion.13), kind=kOutput, calls=%fused_computation.12 | convolution fusion | flops 2463105024 | bytes 52303872 | tf_op jit(solution)/shard_map/ihj,jhd->ihd/dot_general | solution.py:102
  752.9 3.7 fusion.40
  757.1 2.0 fusion.44
  759.9 7.7 all-reduce.6
  773.4 17.7 %all-gather.18.cloned.1.call-done = f32[32,128,128]{2,1,0:T(8,128)} async-done(((f32[8,128,128]{2,1,0:T(8,128)}), f32[32,128,128]{2,1,0:T(8,128)}) %all-gather.18.cloned.1.call-update) | async-done | bytes 2097168 | tf_op jit(solution)/shard_map/all_gather | solution.py:32
  791.1 2.5 fusion.60
  795.0 3.0 psum.42
  798.0 18.6 %all-reduce.8 = (f32[]{:T(128)}, f32[8]{0:T(128)S(1)}) all-reduce(f32[]{:T(128)} %psum.42, f32[8]{0:T(128)S(1)} %dynamic-update-slice.4), channel_id=1, replica_groups=mesh['grp'=2,'seq_0'=8,'seq_1'=4,'head'=4] {'seq_0'}, use_global_device_ids=true, to_apply=%region_19.20 | all-reduce | flops 9 | bytes 72 | tf_op jit(solution)/shard_map/psum | solution.py:43
  827.7 1.9 add_select_fusion
  829.7 3.1 fusion.34
  832.8 2.9 fusion.21
  836.0 1.3 convolution_bitcast_fusion
  838.5 12.0 %all-gather.2 = f32[32,128]{1,0:T(8,128)S(1)} all-gather(f32[8,128]{1,0:T(8,128)S(1)} %bitcast.227), channel_id=4, replica_groups=mesh['grp'=2,'seq_0'=8,'seq_1'=4,'head'=4] {'seq_1'}, dimensions={0}, use_global_device_ids=true | all-gather | bytes 20480 | tf_op jit(solution)/shard_map/all_gather | solution.py:32
  850.6 24.7 %all_gather.84 = f32[8,8,128]{2,1,0:T(8,128)S(1)} all-gather(f32[1,8,128]{2,1,0:T(8,128)S(1)} %fusion.230), channel_id=1, replica_groups=mesh['grp'=2,'seq_0'=8,'seq_1'=4,'head'=4] {'seq_0'}, dimensions={0}, use_global_device_ids=true | all-gather | bytes 36864 | tf_op jit(solution)/shard_map/all_gather | solution.py:32
  876.0 1.3 fusion.85
  877.3 4.2 fusion.19
  883.3 71.1 %all-reduce.12.cloned.1.call-done = f32[8,128,128]{1,2,0:T(8,128)} async-done(((f32[8,128,128]{1,2,0:T(8,128)}), f32[8,128,128]{1,2,0:T(8,128)}) %all-reduce.12.cloned.1.call-update) | async-done | bytes 524304 | tf_op jit(solution)/shard_map/psum | solution.py:43
  954.5 11.1 %psum.44 = f32[]{:T(128)} all-reduce(f32[]{:T(128)} %get-tuple-element.20), channel_id=1, replica_groups=mesh['grp'=2,'seq_0'=8,'seq_1'=4,'head'=4] {'seq_1'}, use_global_device_ids=true, to_apply=%region_20.21 | all-reduce | flops 1 | bytes 8 | tf_op jit(solution)/shard_map/psum | solution.py:43
  965.5 9.2 psum.45
  976.8 26.5 %all-reduce.14.cloned.1.call-done = f32[8,128,128]{1,2,0:T(8,128)} async-done(((f32[8,128,128]{1,2,0:T(8,128)}), f32[8,128,128]{1,2,0:T(8,128)}) %all-reduce.14.cloned.1.call-update) | async-done | bytes 524304 | tf_op jit(solution)/shard_map/psum | solution.py:43
  1003.3 2.0 copy.59
  (173 shorter events, 29.0 us)
Async XLA Ops:
  7.2 613.1 %copy-start = (bf16[192,8,128]{2,1,0:T(8,128)(2,1)S(1)}, bf16[192,8,128]{2,1,0:T(8,128)(2,1)}, u32[]{:S(2)}) copy-start(bf16[192,8,128]{2,1,0:T(8,128)(2,1)} %param.5) | copy-start | bytes 1179652
  7.2 21.4 %copy-start.24 = (bf16[192,8,128]{2,1,0:T(8,128)(2,1)S(1)}, bf16[192,8,128]{2,1,0:T(8,128)(2,1)}, u32[]{:S(2)}) copy-start(bf16[192,8,128]{2,1,0:T(8,128)(2,1)} %param.7) | copy-start | bytes 1179652
  7.2 60.5 %all-gather.16.cloned.1.call-start = ((), (), s32[]{:S(2)}) async-start(), calls=%async_computation.6 | async-start | bytes 2621440 | tf_op jit(solution)/shard_map/all_gather | solution.py:32
  8.4 20.4 %copy-start.19 = (bf16[192,8,128]{2,0,1:T(8,128)(2,1)}, bf16[192,8,128]{2,0,1:T(8,128)(2,1)S(1)}, u32[]{:S(2)}) copy-start(bf16[192,8,128]{2,0,1:T(8,128)(2,1)S(1)} %copy.34) | copy-start | bytes 1179652
  8.4 15.0 %collective-permute-start.2 = (bf16[64,8,128]{2,0,1:T(8,128)(2,1)S(1)}, bf16[64,8,128]{2,0,1:T(8,128)(2,1)S(1)}, u32[]{:S(2)}, u32[]{:S(2)}) collective-permute-start(bf16[64,8,128]{2,0,1:T(8,128)(2,1)S(1)} %slice.344), channel_id=1, source_target_pairs={{0,4},{4,8},{8,12},{12,16},{16,20},{20,24},{24,28},{28,32},{32,36}... | collective-permute-start | bytes 393224 | tf_op jit(solution)/shard_map/ppermute | solution.py:18
  12.6 15.9 %copy-start.31 = (f32[192]{0:T(256)}, f32[192]{0:T(256)S(1)}, u32[]{:S(2)}) copy-start(f32[192]{0:T(256)S(1)} %get-tuple-element.31) | copy-start | bytes 2308
  12.6 10.1 collective-permute-start.1
  17.1 11.5 %collective-permute-start = (bf16[64,8,128]{2,0,1:T(8,128)(2,1)S(1)}, bf16[64,8,128]{2,0,1:T(8,128)(2,1)S(1)}, u32[]{:S(2)}, u32[]{:S(2)}) collective-permute-start(bf16[64,8,128]{2,0,1:T(8,128)(2,1)S(1)} %slice.343), channel_id=1, source_target_pairs={{0,4},{4,8},{8,12},{12,16},{16,20},{20,24},{24,28},{28,32},{32,36}... | collective-permute-start | bytes 393224 | tf_op jit(solution)/shard_map/ppermute | solution.py:18
  22.8 5.7 copy-start.35
  23.4 8.4 copy-start.33
  27.6 1.1 copy-start.7
  28.7 42.3 %copy-start.20 = (bf16[256,8,128]{2,0,1:T(8,128)(2,1)}, bf16[256,8,128]{2,0,1:T(8,128)(2,1)S(1)}, u32[]{:S(2)}) copy-start(bf16[256,8,128]{2,0,1:T(8,128)(2,1)S(1)} %constant_dynamic-update-slice_fusion) | copy-start | bytes 1572868
  29.3 1.0 copy-start.5
  31.9 643.8 %all-gather.12.cloned.1.call-start = ((), (), s32[]{:S(2)}) async-start(), calls=%async_computation.2 | async-start | bytes 4718592 | tf_op jit(solution)/shard_map/all_gather | solution.py:32
  70.2 612.7 %all-gather.10.cloned.1.call-start = ((), (), s32[]{:S(2)}) async-start(), calls=%async_computation.1 | async-start | bytes 12976128 | tf_op jit(solution)/shard_map/all_gather | solution.py:85
  78.6 8.9 copy-start.39
  78.6 402.4 %copy-start.38 = (u32[256]{0:T(256)S(1)}, u32[256]{0:T(256)}, u32[]{:S(2)}) copy-start(u32[256]{0:T(256)} %constant.88) | copy-start | bytes 3076
  78.6 541.7 %copy-start.37 = (s32[192]{0:T(256)S(1)}, s32[192]{0:T(256)}, u32[]{:S(2)}) copy-start(s32[192]{0:T(256)} %param.8) | copy-start | bytes 2308
  78.6 541.7 %copy-start.6 = (f32[8,128,128]{2,1,0:T(8,128)S(1)}, f32[8,128,128]{2,1,0:T(8,128)}, u32[]{:S(2)}) copy-start(f32[8,128,128]{2,1,0:T(8,128)} %param.9) | copy-start | bytes 1572868
  78.6 640.9 %all-to-all-start = ((bf16[32,192,8,128]{3,1,2,0:T(8,128)(2,1)}), bf16[32,192,8,128]{3,1,2,0:T(8,128)(2,1)}, u32[]{:S(2)}, u32[]{:S(2)}) async-start(bf16[32,192,8,128]{3,1,2,0:T(8,128)(2,1)} %stack.2), calls=%async_computation | async-start | bytes 25165824 | tf_op jit(solution)/shard_map/all_to_all | solution.py:87
  87.5 536.5 %copy-start.32 = (f32[192]{0:T(256)S(1)}, f32[192]{0:T(256)}, u32[]{:S(2)}) copy-start(f32[192]{0:T(256)} %copy-done.31) | copy-start | bytes 2308
  87.5 537.5 %copy-start.36 = (f32[256]{0:T(256)S(1)}, f32[256]{0:T(256)}, u32[]{:S(2)}) copy-start(f32[256]{0:T(256)} %copy-done.35) | copy-start | bytes 3076
  87.5 537.6 %copy-start.34 = (f32[192]{0:T(256)S(1)}, f32[192]{0:T(256)}, u32[]{:S(2)}) copy-start(f32[192]{0:T(256)} %copy-done.33) | copy-start | bytes 2308
  87.5 703.6 %all-gather.18.cloned.1.call-start = ((), (), s32[]{:S(2)}) async-start(), calls=%async_computation.7 | async-start | bytes 2621440 | tf_op jit(solution)/shard_map/all_gather | solution.py:32
  622.1 0.9 copy-start.11
  668.8 1.0 copy-start.15
  669.7 0.8 copy-start.17
  669.8 2.8 copy-start.1
  669.8 2.8 copy-start.2
  679.4 0.8 copy-start.3
  731.3 21.6 %copy-start.21 = (bf16[256,8,128]{2,0,1:T(8,128)(2,1)S(1)}, bf16[256,8,128]{2,0,1:T(8,128)(2,1)}, u32[]{:S(2)}) copy-start(bf16[256,8,128]{2,0,1:T(8,128)(2,1)} %copy-done.20) | copy-start | bytes 1572868
  731.3 21.6 %copy-start.25 = (f32[8,192,256]{2,1,0:T(8,128)S(1)}, f32[8,192,256]{2,1,0:T(8,128)}, u32[]{:S(2)}) copy-start(f32[8,192,256]{2,1,0:T(8,128)} %get-tuple-element.69) | copy-start | bytes 4718596
  731.3 21.6 %copy-start.26 = (f32[8,128,192]{1,2,0:T(8,128)S(1)}, f32[8,128,192]{1,2,0:T(8,128)}, u32[]{:S(2)}) copy-start(f32[8,128,192]{1,2,0:T(8,128)} %convolution_multiply_fusion.1) | copy-start | bytes 2359300
  752.8 3.7 copy-start.27
  759.1 118.2 %all-gather.14.cloned.1.call-start = ((), (), s32[]{:S(2)}) async-start(), calls=%async_computation.3 | async-start | bytes 4718592 | tf_op jit(solution)/shard_map/all_gather | solution.py:32
  793.6 160.9 %all-reduce.12.cloned.1.call-start = ((), (), s32[]{:S(2)}) async-start(), calls=%async_computation.4 | async-start | bytes 1048576 | tf_op jit(solution)/shard_map/psum | solution.py:43
  829.7 6.1 copy-start.12
  829.7 6.1 copy-start.14
  832.8 4.5 copy-start.16
  832.8 4.5 copy-start.18
  875.3 2.0 copy-start.22
  875.3 2.0 copy-start.23
  877.2 4.3 copy-start.8
  877.2 4.3 copy-start.10
  881.5 1.0 copy-start.30
  881.7 93.0 %copy-start.29 = (bf16[192,8,128]{2,0,1:T(8,128)(2,1)S(1)}, bf16[192,8,128]{2,0,1:T(8,128)(2,1)}, u32[]{:S(2)}) copy-start(bf16[192,8,128]{2,0,1:T(8,128)(2,1)} %get-tuple-element.22) | copy-start | bytes 1179652
  881.7 94.0 %copy-start.28 = (bf16[192,8,128]{2,0,1:T(8,128)(2,1)S(1)}, bf16[192,8,128]{2,0,1:T(8,128)(2,1)}, u32[]{:S(2)}) copy-start(bf16[192,8,128]{2,0,1:T(8,128)(2,1)} %get-tuple-element.25) | copy-start | bytes 1179652
  883.3 120.0 %all-reduce.14.cloned.1.call-start = ((), (), s32[]{:S(2)}) async-start(), calls=%async_computation.5 | async-start | bytes 1048576 | tf_op jit(solution)/shard_map/psum | solution.py:43
  (3 other events, 2.4 us)
Sparse Core Ops, SparseCore 0:
  32.0 35.6 all-gather.15
  70.3 134.1 all-gather.11
  207.6 271.7 all-gather.9
  759.2 31.8 all-gather.17
  793.7 55.0 all-gather.13
  883.4 71.0 all-reduce.11
  956.8 46.4 all-reduce.13
